TPU v7x, 512 devices: a whole 4x4x16 slice. The times are simulated.
512 devices in a mesh: seq: 128 (over x, z, core), head: 4 (over y).
Axes of the slice: x: 4, y: 4, z: 16, core: 2. Of those that a mesh axis runs over, the one named last changes fastest.
Arguments:
- queries: bfloat16 [65536, 2048], P('seq', 'head'), may hold values from -6 to 6
- keys: bfloat16 [65536, 2048], P('seq', 'head'), may hold values from -6 to 6
- values: bfloat16 [65536, 2048], P('seq', 'head'), may hold values from -6 to 6
- summary_lists: int32 [128, 8, 16], P('seq', 'head'), may hold values from 0 to 126, as said below
- out_weight: bfloat16 [2048, 2048], P('head'), may hold values from -0.125 to 0.125
Outputs:
- mixed: bfloat16 [65536, 2048], P(('seq', 'head'))
Inputs may be any that keep to these rules, and one draw needn't show every extreme that they name: `summary_lists`: entry [b, f, k] names a block. In every query block b above 0 it is below b, and entry [b, f, 0] is b - 1; in query block 0 every entry is 0 and names nothing. Entries may repeat.
All inputs are finite; a program needn't handle non-finite values.
Results may differ from a plain program's by a relative error of at most 0.014.
Values may be sent and summed in bfloat16 or wider, within the bound.
A program may use at most 64 MiB of HBM per device.

v0:
```python
import math
import jax
import jax.numpy as jnp
from jax import lax
from jax.sharding import PartitionSpec as P

HEAD_DIM = 128
BLK = 512
SUMMARY = 32
ROWS_DEV = 1
NEG = -1e30


def softmax_rounded(scores, valid):
    scores = jnp.where(valid, scores, NEG)
    peak = jnp.max(scores, axis=-1, keepdims=True)
    weights = jnp.where(valid, jnp.exp(scores - peak), 0.0)
    return (weights / jnp.sum(weights, axis=-1, keepdims=True)).astype(jnp.bfloat16)


def column_attend(pieces):
    col_q, col_k, col_v = pieces
    scale = HEAD_DIM ** (-0.5)
    scores = jnp.einsum("rxcd,sxcd->xcrs", col_q, col_k, preferred_element_type=jnp.float32) * scale
    blocks = col_q.shape[0]
    earlier = jnp.arange(blocks)[:, None] >= jnp.arange(blocks)[None, :]
    weights = softmax_rounded(scores, earlier)
    return jnp.einsum("xcrs,sxcd->rxcd", weights, col_v, preferred_element_type=jnp.float32).astype(
        jnp.bfloat16
    )


def absorb(state, scores, multiplier):
    old_peak, old_denom = (state[0], state[1])
    new_peak = jnp.maximum(old_peak, jnp.max(scores, axis=(3, 4)))
    weights = jnp.exp(scores - new_peak[..., None, None]) * multiplier[:, :, None, :, None]
    shrink = jnp.exp(old_peak - new_peak)
    return (new_peak, old_denom * shrink + jnp.sum(weights, axis=(3, 4)), shrink, weights)


def per_device(queries, keys, values, summary_lists, out_weight):
    scale = HEAD_DIM ** (-0.5)
    seq_count = lax.axis_size("seq")
    query_heads = queries.reshape(ROWS_DEV, BLK, 4, HEAD_DIM)
    key_heads = keys.reshape(ROWS_DEV, BLK, 4, HEAD_DIM)
    value_heads = values.reshape(ROWS_DEV, BLK, 4, HEAD_DIM)
    causal = jnp.arange(BLK)[:, None] >= jnp.arange(BLK)[None, :]
    block_index = lax.axis_index("seq") * ROWS_DEV + jnp.arange(ROWS_DEV, dtype=jnp.int32)

    def column_layout(source):
        return source[:, :, 1].reshape(ROWS_DEV, seq_count, BLK // seq_count, HEAD_DIM)

    column_moved = column_attend(
        (
            lax.all_to_all(
                column_layout(query_heads), "seq", split_axis=1, concat_axis=0, tiled=True
            ),
            lax.all_to_all(
                column_layout(key_heads), "seq", split_axis=1, concat_axis=0, tiled=True
            ),
            lax.all_to_all(
                column_layout(value_heads), "seq", split_axis=1, concat_axis=0, tiled=True
            ),
        )
    )
    row_scores = (
        jnp.einsum(
            "rid,rjd->rij",
            query_heads[:, :, 0],
            key_heads[:, :, 0],
            preferred_element_type=jnp.float32,
        )
        * scale
    )
    row_weights = softmax_rounded(row_scores, causal)
    row_out = jnp.einsum(
        "rij,rjd->rid", row_weights, value_heads[:, :, 0], preferred_element_type=jnp.float32
    ).astype(jnp.bfloat16)
    fixed_q = query_heads[:, :, 2:]
    fixed_k = key_heads[:, :, 2:]
    fixed_v = value_heads[:, :, 2:]
    own_scores = (
        jnp.einsum("rifd,rjfd->rfij", fixed_q, fixed_k, preferred_element_type=jnp.float32) * scale
    )
    own_scores = jnp.where(causal, own_scores, NEG)
    own_peak = jnp.max(own_scores, axis=-1)
    own_weights = jnp.exp(own_scores - own_peak[..., None])
    own_denom = jnp.sum(own_weights, axis=-1)
    own_sum = jnp.einsum(
        "rfij,rjfd->rfid",
        own_weights.astype(jnp.bfloat16),
        fixed_v,
        preferred_element_type=jnp.float32,
    )
    tail_k = jnp.swapaxes(fixed_k[:, BLK - SUMMARY :], 1, 2)
    tail_v = jnp.swapaxes(fixed_v[:, BLK - SUMMARY :], 1, 2)
    piece_k = lax.all_gather(tail_k, "seq", axis=0, tiled=True)
    piece_v = lax.all_gather(tail_v, "seq", axis=0, tiled=True)
    arrived = piece_k.shape[0]
    stride = math.gcd(arrived, 8)

    def inner(turn, running):
        offset = turn * stride
        part_k = lax.dynamic_slice_in_dim(piece_k, offset, stride, 0)
        part_v = lax.dynamic_slice_in_dim(piece_v, offset, stride, 0)
        tile_index = offset + jnp.arange(stride, dtype=jnp.int32)
        matches = (summary_lists[:, :, :, None] == tile_index) & (
            tile_index < block_index[:, None, None, None]
        )
        multiplier = jnp.sum(matches.astype(jnp.float32), axis=2)
        scores = (
            jnp.einsum("rifd,nfcd->rfinc", fixed_q, part_k, preferred_element_type=jnp.float32)
            * scale
        )
        scores = jnp.where(multiplier[:, :, None, :, None] > 0, scores, NEG)
        new_peak, new_denom, shrink, weights = absorb(running, scores, multiplier)
        new_sum = running[2] * shrink[..., None] + jnp.einsum(
            "rfinc,nfcd->rfid",
            weights.astype(jnp.bfloat16),
            part_v,
            preferred_element_type=jnp.float32,
        )
        return (new_peak, new_denom, new_sum)

    final_peak, final_denom, final_sum = lax.fori_loop(
        0, arrived // stride, inner, (own_peak, own_denom, own_sum)
    )
    fixed_out = jnp.swapaxes((final_sum / final_denom[..., None]).astype(jnp.bfloat16), 1, 2)
    column_out = lax.all_to_all(
        column_moved, "seq", split_axis=0, concat_axis=1, tiled=True
    ).reshape(ROWS_DEV, BLK, HEAD_DIM)
    attended = jnp.concatenate(
        [row_out[:, :, None], column_out[:, :, None], fixed_out], axis=2
    ).reshape(ROWS_DEV * BLK, 4 * HEAD_DIM)
    return lax.psum_scatter(
        jnp.dot(attended, out_weight, preferred_element_type=jnp.float32).astype(jnp.bfloat16),
        "head",
        scatter_dimension=0,
        tiled=True,
    )


def solution(mesh):
    return jax.shard_map(
        per_device,
        mesh=mesh,
        in_specs=(
            P("seq", "head"),
            P("seq", "head"),
            P("seq", "head"),
            P("seq", "head", None),
            P("head", None),
        ),
        out_specs=P(("seq", "head"), None),
        check_vma=False,
    )
```

profile of v0, /device:TPU:1, one launch (start us, length us, event | category | flops | bytes accessed | tf_op | source)
XLA Modules:
  0.0 376.9 jit_solution(72792832093655614)
XLA Ops:
  6.5 1.4 copy.55
  8.1 0.8 copy.72
  8.9 1.3 copy.56
  10.2 0.7 copy.73
  11.0 1.3 copy.54
  12.2 0.7 copy.57
  13.0 20.4 %all-to-all-start = ((bf16[1,128,4,128]{3,2,0,1:T(4,128)(2,1)}), bf16[1,128,4,128]{3,2,0,1:T(4,128)(2,1)S(1)}, u32[]{:S(2)}, u32[]{:S(2)}) async-start(bf16[1,128,4,128]{3,2,0,1:T(4,128)(2,1)} %bitcast.23), calls=%async_computation | async-start | bytes 262144 | tf_op jit(solution)/shard_map/all_to_all | solution.py:55
  33.4 0.7 copy.60
  34.1 1.3 fusion.47
  35.5 15.8 %all-to-all-done = bf16[1,128,4,128]{3,2,0,1:T(4,128)(2,1)S(1)} async-done(((bf16[1,128,4,128]{3,2,0,1:T(4,128)(2,1)}), bf16[1,128,4,128]{3,2,0,1:T(4,128)(2,1)S(1)}, u32[]{:S(2)}, u32[]{:S(2)}) %all-to-all-start) | async-done | bytes 131104 | tf_op jit(solution)/shard_map/all_to_all | solution.py:55
  51.3 6.7 %all-to-all-start.1 = ((bf16[1,128,4,128]{3,2,0,1:T(4,128)(2,1)}), bf16[1,128,4,128]{3,2,0,1:T(4,128)(2,1)S(1)}, u32[]{:S(2)}, u32[]{:S(2)}) async-start(bf16[1,128,4,128]{3,2,0,1:T(4,128)(2,1)} %bitcast.26), calls=%async_computation.1 | async-start | bytes 262144 | tf_op jit(solution)/shard_map/all_to_all | solution.py:58
  58.1 0.9 slice.51
  59.0 0.8 copy.63
  59.8 1.4 fusion.30
  61.1 2.9 fusion.15
  64.0 11.7 %all-to-all-done.1 = bf16[1,128,4,128]{3,2,0,1:T(4,128)(2,1)S(1)} async-done(((bf16[1,128,4,128]{3,2,0,1:T(4,128)(2,1)}), bf16[1,128,4,128]{3,2,0,1:T(4,128)(2,1)S(1)}, u32[]{:S(2)}, u32[]{:S(2)}) %all-to-all-start.1) | async-done | bytes 131104 | tf_op jit(solution)/shard_map/all_to_all | solution.py:58
  75.7 6.7 %all-to-all-start.2 = ((bf16[1,128,4,128]{3,2,0,1:T(4,128)(2,1)}), bf16[1,128,4,128]{3,2,0,1:T(4,128)(2,1)S(1)}, u32[]{:S(2)}, u32[]{:S(2)}) async-start(bf16[1,128,4,128]{3,2,0,1:T(4,128)(2,1)} %bitcast.29), calls=%async_computation.2 | async-start | bytes 262144 | tf_op jit(solution)/shard_map/all_to_all | solution.py:61
  82.5 0.6 iota_compare_fusion.1
  83.3 2.3 fusion.23
  85.8 14.3 %all-to-all-done.2 = bf16[1,128,4,128]{3,2,0,1:T(4,128)(2,1)S(1)} async-done(((bf16[1,128,4,128]{3,2,0,1:T(4,128)(2,1)}), bf16[1,128,4,128]{3,2,0,1:T(4,128)(2,1)S(1)}, u32[]{:S(2)}, u32[]{:S(2)}) %all-to-all-start.2) | async-done | bytes 131104 | tf_op jit(solution)/shard_map/all_to_all | solution.py:61
  100.4 0.8 copy.67
  101.1 6.8 %all-to-all-start.3 = ((bf16[128,1,4,128]{3,2,1,0:T(4,128)(2,1)}), bf16[128,1,4,128]{3,2,1,0:T(4,128)(2,1)S(1)}, u32[]{:S(2)}, u32[]{:S(2)}) async-start(bf16[128,1,4,128]{3,2,1,0:T(4,128)(2,1)} %copy.67), calls=%async_computation.3 | async-start | bytes 262144 | tf_op jit(solution)/shard_map/all_to_all | solution.py:129
  108.2 2.2 fusion.17
  110.4 1.7 convolution_bitcast_fusion.1
  112.1 13.7 %all-to-all-done.3 = bf16[128,1,4,128]{3,2,1,0:T(4,128)(2,1)S(1)} async-done(((bf16[128,1,4,128]{3,2,1,0:T(4,128)(2,1)}), bf16[128,1,4,128]{3,2,1,0:T(4,128)(2,1)S(1)}, u32[]{:S(2)}, u32[]{:S(2)}) %all-to-all-start.3) | async-done | bytes 131104 | tf_op jit(solution)/shard_map/all_to_all | solution.py:129
  125.9 32.0 %all-gather.3.cloned.1.call-done = bf16[128,2,32,128]{3,2,1,0:T(8,128)(2,1)} async-done(((bf16[1,2,32,128]{3,2,1,0:T(8,128)(2,1)}), bf16[128,2,32,128]{3,2,1,0:T(8,128)(2,1)}) %all-gather.3.cloned.1.call-update) | async-done | bytes 2097168 | tf_op jit(solution)/shard_map/all_gather | solution.py:97
  157.9 140.1 %all-gather.5.cloned.1.call-done = bf16[128,2,32,128]{3,2,1,0:T(8,128)(2,1)} async-done(((bf16[1,2,32,128]{3,2,1,0:T(8,128)(2,1)}), bf16[128,2,32,128]{3,2,1,0:T(8,128)(2,1)}) %all-gather.5.cloned.1.call-update) | async-done | bytes 2097168 | tf_op jit(solution)/shard_map/all_gather | solution.py:98
  298.1 36.2 %while.17 = (s32[]{:T(128)}, f32[1,2,512]{2,1,0:T(2,128)S(1)}, f32[1,2,512]{2,1,0:T(2,128)S(1)}, f32[1,2,512,128]{2,3,1,0:T(8,128)S(1)}, s32[1,2,16]{2,1,0:T(2,1...) while((s32[]{:T(128)}, f32[1,2,512]{2,1,0:T(2,128)S(1)}, ...), condition=%wide.region_10.11_spmd, body=%wide.region_6.10_spmd.sunk | while | flops 136843296 | bytes 5309099 | solution.py:125
  298.1 1.0 constant_dynamic-slice_fusion.3
  299.6 0.4 fusion.65
  300.3 1.0 constant_dynamic-slice_fusion.3
  302.6 1.0 constant_dynamic-slice_fusion.3
  304.9 1.0 constant_dynamic-slice_fusion.3
  307.1 1.0 constant_dynamic-slice_fusion.3
  308.6 0.4 fusion.65
  309.4 1.0 constant_dynamic-slice_fusion.3
  311.6 1.0 constant_dynamic-slice_fusion.3
  313.9 1.0 constant_dynamic-slice_fusion.3
  316.2 1.0 constant_dynamic-slice_fusion.3
  318.4 1.0 constant_dynamic-slice_fusion.3
  320.7 1.0 constant_dynamic-slice_fusion.3
  322.9 1.0 constant_dynamic-slice_fusion.3
  325.2 1.0 constant_dynamic-slice_fusion.3
  327.4 1.0 constant_dynamic-slice_fusion.3
  329.7 1.0 constant_dynamic-slice_fusion.3
  332.0 1.0 constant_dynamic-slice_fusion.3
  334.4 2.6 convolution_convert_fusion
  337.0 33.4 %reduce-scatter.2.cloned.1.call-done = bf16[128,2048]{1,0:T(8,128)(2,1)} async-done(((bf16[512,2048]{1,0:T(8,128)(2,1)}), bf16[128,2048]{1,0:T(8,128)(2,1)}) %reduce-scatter.2.cloned.1.call-update) | async-done | bytes 524304 | tf_op jit(solution)/shard_map/reduce_scatter | solution.py:135
  (190 shorter events, 19.9 us)
Async XLA Ops:
  6.5 327.8 %copy-start = (bf16[512,2048]{1,0:T(8,128)(2,1)S(1)}, bf16[512,2048]{1,0:T(8,128)(2,1)}, u32[]{:S(2)}) copy-start(bf16[512,2048]{1,0:T(8,128)(2,1)} %param.11) | copy-start | bytes 6291460
  6.5 151.4 %all-gather.3.cloned.1.call-start = ((), (), s32[]{:S(2)}) async-start(), calls=%async_computation.5 | async-start | bytes 2113536 | tf_op jit(solution)/shard_map/all_gather | solution.py:97
  7.9 27.5 %copy-start.3 = (bf16[512,512]{0,1:T(8,128)(2,1)}, bf16[512,512]{0,1:T(8,128)(2,1)S(1)}, u32[]{:S(2)}) copy-start(bf16[512,512]{0,1:T(8,128)(2,1)S(1)} %copy.55) | copy-start | bytes 1572868
  8.8 289.2 %all-gather.5.cloned.1.call-start = ((), (), s32[]{:S(2)}) async-start(), calls=%async_computation.6 | async-start | bytes 2113536 | tf_op jit(solution)/shard_map/all_gather | solution.py:98
  10.1 0.8 copy-start.2
  13.0 38.3 %all-to-all-start = ((bf16[1,128,4,128]{3,2,0,1:T(4,128)(2,1)}), bf16[1,128,4,128]{3,2,0,1:T(4,128)(2,1)S(1)}, u32[]{:S(2)}, u32[]{:S(2)}) async-start(bf16[1,128,4,128]{3,2,0,1:T(4,128)(2,1)} %bitcast.23), calls=%async_computation | async-start | bytes 262144 | tf_op jit(solution)/shard_map/all_to_all | solution.py:55
  51.3 24.4 %all-to-all-start.1 = ((bf16[1,128,4,128]{3,2,0,1:T(4,128)(2,1)}), bf16[1,128,4,128]{3,2,0,1:T(4,128)(2,1)S(1)}, u32[]{:S(2)}, u32[]{:S(2)}) async-start(bf16[1,128,4,128]{3,2,0,1:T(4,128)(2,1)} %bitcast.26), calls=%async_computation.1 | async-start | bytes 262144 | tf_op jit(solution)/shard_map/all_to_all | solution.py:58
  75.7 24.4 %all-to-all-start.2 = ((bf16[1,128,4,128]{3,2,0,1:T(4,128)(2,1)}), bf16[1,128,4,128]{3,2,0,1:T(4,128)(2,1)S(1)}, u32[]{:S(2)}, u32[]{:S(2)}) async-start(bf16[1,128,4,128]{3,2,0,1:T(4,128)(2,1)} %bitcast.29), calls=%async_computation.2 | async-start | bytes 262144 | tf_op jit(solution)/shard_map/all_to_all | solution.py:61
  83.3 2.3 copy-start.6
  101.1 24.7 %all-to-all-start.3 = ((bf16[128,1,4,128]{3,2,1,0:T(4,128)(2,1)}), bf16[128,1,4,128]{3,2,1,0:T(4,128)(2,1)S(1)}, u32[]{:S(2)}, u32[]{:S(2)}) async-start(bf16[128,1,4,128]{3,2,1,0:T(4,128)(2,1)} %copy.67), calls=%async_computation.3 | async-start | bytes 262144 | tf_op jit(solution)/shard_map/all_to_all | solution.py:129
  107.9 262.5 %reduce-scatter.2.cloned.1.call-start = ((), (), s32[]{:S(2)}) async-start(), calls=%async_computation.7 | async-start | bytes 2621440 | tf_op jit(solution)/shard_map/reduce_scatter | solution.py:135
  108.2 2.2 copy-start.1
  110.4 187.6 %copy-start.5 = (s32[1,2,16]{2,1,0:T(2,128)S(1)}, s32[1,2,16]{2,1,0:T(2,128)}, u32[]{:S(2)}) copy-start(s32[1,2,16]{2,1,0:T(2,128)} %param.10) | copy-start | bytes 388
  298.1 36.2 %copy-start.4 = (bf16[1,512,1,128]{1,3,2,0:T(8,128)(2,1)S(1)}, bf16[1,512,1,128]{1,3,2,0:T(8,128)(2,1)}, u32[]{:S(2)}) copy-start(bf16[1,512,1,128]{1,3,2,0:T(8,128)(2,1)} %fusion.23) | copy-start | bytes 393220
Sparse Core Ops, SparseCore 0:
  10.5 147.4 all-gather.2
  161.1 136.9 all-gather.4
  337.1 33.2 reduce-scatter.1
where the time goes:
time: 378 us; the launch traced here: 377 us
  waiting for transfers between devices  261 us (69%)
  starting transfers between devices  40.9 us (11%)
  local copies, waits for them, and re-layouts  25.7 us (7%)
  matrix products  23.2 us (6%)
  between operations  13.3 us (4%)
  other arithmetic  11.7 us (3%)
    all_gather x1, waiting for transfers between devices, per_device(): piece_v = lax.all_gather(tail_v, 'seq', axis=0, tiled=True)  140 us
    reduce_scatter x1, waiting for transfers between devices, per_device(): lax.psum_scatter(jnp.dot(attended, out_weight, preferred_element_type=jnp...  33.4 us
    all_gather x1, waiting for transfers between devices, per_device(): piece_k = lax.all_gather(tail_k, 'seq', axis=0, tiled=True)  32 us
    all_to_all x1, starting transfers between devices, per_device(): lax.all_to_all(column_layout(query_heads), 'seq', split_axis=1, concat_ax...  20.4 us
    dynamic_slice x16, local copies, waits for them, and re-layouts, inner(): part_v = lax.dynamic_slice_in_dim(piece_v, offset, stride, 0)  15.9 us
    all_to_all x1, waiting for transfers between devices, per_device(): lax.all_to_all(column_layout(query_heads), 'seq', split_axis=1, concat_ax...  15.8 us
    all_to_all x1, waiting for transfers between devices, per_device(): lax.all_to_all(column_layout(value_heads), 'seq', split_axis=1, concat_ax...  14.3 us
    all_to_all x1, waiting for transfers between devices, per_device(): lax.all_to_all(column_moved, 'seq', split_axis=0, concat_axis=1, tiled=True)  13.7 us
  transfers between devices with their start and end apart: 7, of which 7 were waited for; matrix products, arithmetic and copies ran while one was open for 5% of the time, Pallas kernels for 0%

commit v1 on v0

--- a/solution.py
+++ b/solution.py
@@ -94,8 +94,11 @@
     )
     tail_k = jnp.swapaxes(fixed_k[:, BLK - SUMMARY :], 1, 2)
     tail_v = jnp.swapaxes(fixed_v[:, BLK - SUMMARY :], 1, 2)
-    piece_k = lax.all_gather(tail_k, "seq", axis=0, tiled=True)
-    piece_v = lax.all_gather(tail_v, "seq", axis=0, tiled=True)
+    piece_k, piece_v = jnp.split(
+        lax.all_gather(jnp.concatenate([tail_k, tail_v], axis=1), "seq", axis=0, tiled=True),
+        [tail_k.shape[1]],
+        axis=1,
+    )
     arrived = piece_k.shape[0]
     stride = math.gcd(arrived, 8)
 

time: 378 us -> 245 us (0.65)
  waiting for transfers between devices: 261 us -> 123 us
  local copies, waits for them, and re-layouts: 25.7 us -> 29.8 us
    all_gather x2 -> x1, waiting for transfers between devices: 172 us -> 32.5 us  [per_device(): lax.all_gather(jnp.concatenate([tail_k, tail_v], axis=1), 'seq', axis=0,...]
    split x0 -> x1, local copies, waits for them, and re-layouts: none -> 5.18 us  [per_device(): jnp.split(lax.all_gather(jnp.concatenate([tail_k, tail_v], axis=1), 'seq'...]
  transfers between devices with their start and end apart: 7 -> 6, of which waited for: 7 -> 6; matrix products, arithmetic and copies ran while one was open for 5% -> 8% of each run, Pallas kernels for 0% -> 0%
where the time goes in v1:
time: 245 us; the launch traced here: 244 us
  waiting for transfers between devices  123 us (50%)
  starting transfers between devices  40.8 us (17%)
  local copies, waits for them, and re-layouts  29.8 us (12%)
  matrix products  23.2 us (9%)
  between operations  13.6 us (6%)
  other arithmetic  12.4 us (5%)
    all_gather x1, waiting for transfers between devices, per_device(): lax.all_gather(jnp.concatenate([tail_k, tail_v], axis=1), 'seq', axis=0,...  32.5 us
    reduce_scatter x1, waiting for transfers between devices, per_device(): lax.psum_scatter(jnp.dot(attended, out_weight, preferred_element_type=jnp...  32.4 us
    all_to_all x1, starting transfers between devices, per_device(): lax.all_to_all(column_layout(query_heads), 'seq', split_axis=1, concat_ax...  20.4 us
    all_to_all x1, waiting for transfers between devices, per_device(): lax.all_to_all(column_layout(query_heads), 'seq', split_axis=1, concat_ax...  16.3 us
    dynamic_slice x16, local copies, waits for them, and re-layouts, inner(): part_v = lax.dynamic_slice_in_dim(piece_v, offset, stride, 0)  15.9 us
    all_to_all x1, waiting for transfers between devices, per_device(): lax.all_to_all(column_moved, 'seq', split_axis=0, concat_axis=1, tiled=True)  15.7 us
    all_to_all x1, waiting for transfers between devices, per_device(): lax.all_to_all(column_layout(value_heads), 'seq', split_axis=1, concat_ax...  14.3 us
    all_to_all x1, waiting for transfers between devices, per_device(): lax.all_to_all(column_layout(key_heads), 'seq', split_axis=1, concat_axis...  11.7 us
  transfers between devices with their start and end apart: 6, of which 6 were waited for; matrix products, arithmetic and copies ran while one was open for 8% of the time, Pallas kernels for 0%

profile of v1, /device:TPU:1, one launch (start us, length us, event | category | flops | bytes accessed | tf_op | source)
XLA Modules:
  0.0 243.8 jit_solution(6792491259600552113)
XLA Ops:
  6.5 1.4 copy.55
  8.0 1.4 copy.56
  9.8 0.6 pad_maximum_fusion.1
  10.4 1.3 copy.54
  11.7 0.7 copy.57
  12.5 20.4 %all-to-all-start = ((bf16[1,128,4,128]{3,2,0,1:T(4,128)(2,1)}), bf16[1,128,4,128]{3,2,0,1:T(4,128)(2,1)S(1)}, u32[]{:S(2)}, u32[]{:S(2)}) async-start(bf16[1,128,4,128]{3,2,0,1:T(4,128)(2,1)} %bitcast.23), calls=%async_computation | async-start | bytes 262144 | tf_op jit(solution)/shard_map/all_to_all | solution.py:55
  32.9 0.8 copy.60
  33.6 1.4 fusion.48
  35.0 16.3 %all-to-all-done = bf16[1,128,4,128]{3,2,0,1:T(4,128)(2,1)S(1)} async-done(((bf16[1,128,4,128]{3,2,0,1:T(4,128)(2,1)}), bf16[1,128,4,128]{3,2,0,1:T(4,128)(2,1)S(1)}, u32[]{:S(2)}, u32[]{:S(2)}) %all-to-all-start) | async-done | bytes 131104 | tf_op jit(solution)/shard_map/all_to_all | solution.py:55
  51.3 6.3 %all-to-all-start.1 = ((bf16[1,128,4,128]{3,2,0,1:T(4,128)(2,1)}), bf16[1,128,4,128]{3,2,0,1:T(4,128)(2,1)S(1)}, u32[]{:S(2)}, u32[]{:S(2)}) async-start(bf16[1,128,4,128]{3,2,0,1:T(4,128)(2,1)} %bitcast.26), calls=%async_computation.1 | async-start | bytes 262144 | tf_op jit(solution)/shard_map/all_to_all | solution.py:58
  57.8 0.9 slice.51
  58.7 0.7 copy.63
  59.4 1.4 fusion.30
  60.8 2.9 %fusion.15 = (f32[2,512]{1,0:T(2,128)S(1)}, f32[2,512,512]{1,2,0:T(8,128)}) fusion(pred[512,512]{0,1:T(8,128)(4,1)S(1)} %iota_compare_fusion, bf16[1,512,4,128]{1,3,2,0:T(8,128)(2,1)} %bitcast.141, bf16[1,512,4,128]{1,3,2,0:T(8,128)(2,1)S(1)} %bitcast.132), kind=kOutput, calls=%fused_computation.29 | convolution fusion | flops 135789568 | bytes 2887680 | tf_op jit(solution)/shard_map/rifd,rjfd->rfij/dot_general | solution.py:83
  63.7 11.7 %all-to-all-done.1 = bf16[1,128,4,128]{3,2,0,1:T(4,128)(2,1)S(1)} async-done(((bf16[1,128,4,128]{3,2,0,1:T(4,128)(2,1)}), bf16[1,128,4,128]{3,2,0,1:T(4,128)(2,1)S(1)}, u32[]{:S(2)}, u32[]{:S(2)}) %all-to-all-start.1) | async-done | bytes 131104 | tf_op jit(solution)/shard_map/all_to_all | solution.py:58
  75.4 7.0 %all-to-all-start.2 = ((bf16[1,128,4,128]{3,2,0,1:T(4,128)(2,1)}), bf16[1,128,4,128]{3,2,0,1:T(4,128)(2,1)S(1)}, u32[]{:S(2)}, u32[]{:S(2)}) async-start(bf16[1,128,4,128]{3,2,0,1:T(4,128)(2,1)} %bitcast.29), calls=%async_computation.2 | async-start | bytes 262144 | tf_op jit(solution)/shard_map/all_to_all | solution.py:61
  82.4 0.6 iota_compare_fusion.1
  83.3 2.3 fusion.23
  85.8 14.3 %all-to-all-done.2 = bf16[1,128,4,128]{3,2,0,1:T(4,128)(2,1)S(1)} async-done(((bf16[1,128,4,128]{3,2,0,1:T(4,128)(2,1)}), bf16[1,128,4,128]{3,2,0,1:T(4,128)(2,1)S(1)}, u32[]{:S(2)}, u32[]{:S(2)}) %all-to-all-start.2) | async-done | bytes 131104 | tf_op jit(solution)/shard_map/all_to_all | solution.py:61
  100.4 0.8 copy.67
  101.1 6.8 %all-to-all-start.3 = ((bf16[128,1,4,128]{3,2,1,0:T(4,128)(2,1)}), bf16[128,1,4,128]{3,2,1,0:T(4,128)(2,1)S(1)}, u32[]{:S(2)}, u32[]{:S(2)}) async-start(bf16[128,1,4,128]{3,2,1,0:T(4,128)(2,1)} %copy.67), calls=%async_computation.3 | async-start | bytes 262144 | tf_op jit(solution)/shard_map/all_to_all | solution.py:132
  108.2 2.2 fusion.17
  110.4 1.7 convolution_bitcast_fusion.1
  112.1 15.7 %all-to-all-done.3 = bf16[128,1,4,128]{3,2,1,0:T(4,128)(2,1)S(1)} async-done(((bf16[128,1,4,128]{3,2,1,0:T(4,128)(2,1)}), bf16[128,1,4,128]{3,2,1,0:T(4,128)(2,1)S(1)}, u32[]{:S(2)}, u32[]{:S(2)}) %all-to-all-start.3) | async-done | bytes 131104 | tf_op jit(solution)/shard_map/all_to_all | solution.py:132
  128.0 32.5 %all-gather.2.cloned.1.call-done = bf16[128,4,32,128]{3,2,1,0:T(8,128)(2,1)} async-done(((bf16[1,4,32,128]{3,2,1,0:T(8,128)(2,1)}), bf16[128,4,32,128]{3,2,1,0:T(8,128)(2,1)}) %all-gather.2.cloned.1.call-update) | async-done | bytes 4194320 | tf_op jit(solution)/shard_map/all_gather | solution.py:98
  160.4 5.2 %fusion.46 = (bf16[128,2,32,128]{3,2,1,0:T(8,128)(2,1)}, bf16[128,2,32,128]{3,2,1,0:T(8,128)(2,1)}) fusion(bf16[128,4,32,128]{3,2,1,0:T(8,128)(2,1)} %all-gather.2.cloned.1.call-done), kind=kLoop, calls=%fused_computation.79 | loop fusion | bytes 8388608 | tf_op jit(solution)/shard_map/split | solution.py:97
  165.6 36.1 %while.17 = (s32[]{:T(128)}, f32[1,2,512]{2,1,0:T(2,128)S(1)}, f32[1,2,512]{2,1,0:T(2,128)S(1)}, f32[1,2,512,128]{2,3,1,0:T(8,128)S(1)}, s32[1,2,16]{2,1,0:T(2,1...) while((s32[]{:T(128)}, f32[1,2,512]{2,1,0:T(2,128)S(1)}, ...), condition=%wide.region_10.11_spmd, body=%wide.region_6.10_spmd.sunk | while | flops 136843296 | bytes 5309099 | solution.py:128
  165.6 1.0 constant_dynamic-slice_fusion.3
  167.2 0.4 fusion.66
  167.9 1.0 constant_dynamic-slice_fusion.3
  169.4 0.4 fusion.66
  170.2 1.0 constant_dynamic-slice_fusion.3
  171.7 0.4 fusion.66
  172.4 1.0 constant_dynamic-slice_fusion.3
  174.7 1.0 constant_dynamic-slice_fusion.3
  176.9 1.0 constant_dynamic-slice_fusion.3
  179.2 1.0 constant_dynamic-slice_fusion.3
  181.5 1.0 constant_dynamic-slice_fusion.3
  183.7 1.0 constant_dynamic-slice_fusion.3
  186.0 1.0 constant_dynamic-slice_fusion.3
  188.2 1.0 constant_dynamic-slice_fusion.3
  190.5 1.0 constant_dynamic-slice_fusion.3
  192.7 1.0 constant_dynamic-slice_fusion.3
  195.0 1.0 constant_dynamic-slice_fusion.3
  197.3 1.0 constant_dynamic-slice_fusion.3
  199.5 1.0 constant_dynamic-slice_fusion.3
  201.9 2.6 %convolution_convert_fusion = bf16[512,2048]{1,0:T(8,128)(2,1)} fusion(bf16[512,512]{0,1:T(8,128)(2,1)S(1)} %bitcast.142, bf16[512,2048]{1,0:T(8,128)(2,1)S(1)} %copy-done), kind=kOutput, calls=%fused_computation.26 | convolution fusion | flops 1074790400 | bytes 4718592 | tf_op jit(solution)/shard_map/dot_general | solution.py:139
  204.5 32.4 %reduce-scatter.2.cloned.1.call-done = bf16[128,2048]{1,0:T(8,128)(2,1)} async-done(((bf16[512,2048]{1,0:T(8,128)(2,1)}), bf16[128,2048]{1,0:T(8,128)(2,1)}) %reduce-scatter.2.cloned.1.call-update) | async-done | bytes 524304 | tf_op jit(solution)/shard_map/reduce_scatter | solution.py:138
  (189 shorter events, 19.6 us)
Async XLA Ops:
  6.5 195.4 %copy-start = (bf16[512,2048]{1,0:T(8,128)(2,1)S(1)}, bf16[512,2048]{1,0:T(8,128)(2,1)}, u32[]{:S(2)}) copy-start(bf16[512,2048]{1,0:T(8,128)(2,1)} %param.11) | copy-start | bytes 6291460
  6.5 153.9 %all-gather.2.cloned.1.call-start = ((), (), s32[]{:S(2)}) async-start(), calls=%async_computation.5 | async-start | bytes 4227072 | tf_op jit(solution)/shard_map/all_gather | solution.py:98
  7.9 27.0 %copy-start.3 = (bf16[512,512]{0,1:T(8,128)(2,1)}, bf16[512,512]{0,1:T(8,128)(2,1)S(1)}, u32[]{:S(2)}) copy-start(bf16[512,512]{0,1:T(8,128)(2,1)S(1)} %copy.55) | copy-start | bytes 1572868
  9.4 1.0 copy-start.2
  12.5 38.9 %all-to-all-start = ((bf16[1,128,4,128]{3,2,0,1:T(4,128)(2,1)}), bf16[1,128,4,128]{3,2,0,1:T(4,128)(2,1)S(1)}, u32[]{:S(2)}, u32[]{:S(2)}) async-start(bf16[1,128,4,128]{3,2,0,1:T(4,128)(2,1)} %bitcast.23), calls=%async_computation | async-start | bytes 262144 | tf_op jit(solution)/shard_map/all_to_all | solution.py:55
  51.3 24.1 %all-to-all-start.1 = ((bf16[1,128,4,128]{3,2,0,1:T(4,128)(2,1)}), bf16[1,128,4,128]{3,2,0,1:T(4,128)(2,1)S(1)}, u32[]{:S(2)}, u32[]{:S(2)}) async-start(bf16[1,128,4,128]{3,2,0,1:T(4,128)(2,1)} %bitcast.26), calls=%async_computation.1 | async-start | bytes 262144 | tf_op jit(solution)/shard_map/all_to_all | solution.py:58
  75.4 24.7 %all-to-all-start.2 = ((bf16[1,128,4,128]{3,2,0,1:T(4,128)(2,1)}), bf16[1,128,4,128]{3,2,0,1:T(4,128)(2,1)S(1)}, u32[]{:S(2)}, u32[]{:S(2)}) async-start(bf16[1,128,4,128]{3,2,0,1:T(4,128)(2,1)} %bitcast.29), calls=%async_computation.2 | async-start | bytes 262144 | tf_op jit(solution)/shard_map/all_to_all | solution.py:61
  83.3 2.3 copy-start.6
  101.1 26.7 %all-to-all-start.3 = ((bf16[128,1,4,128]{3,2,1,0:T(4,128)(2,1)}), bf16[128,1,4,128]{3,2,1,0:T(4,128)(2,1)S(1)}, u32[]{:S(2)}, u32[]{:S(2)}) async-start(bf16[128,1,4,128]{3,2,1,0:T(4,128)(2,1)} %copy.67), calls=%async_computation.3 | async-start | bytes 262144 | tf_op jit(solution)/shard_map/all_to_all | solution.py:132
  107.9 129.1 %reduce-scatter.2.cloned.1.call-start = ((), (), s32[]{:S(2)}) async-start(), calls=%async_computation.6 | async-start | bytes 2621440 | tf_op jit(solution)/shard_map/reduce_scatter | solution.py:138
  108.2 2.2 copy-start.1
  127.9 37.7 %copy-start.5 = (s32[1,2,16]{2,1,0:T(2,128)S(1)}, s32[1,2,16]{2,1,0:T(2,128)}, u32[]{:S(2)}) copy-start(s32[1,2,16]{2,1,0:T(2,128)} %param.10) | copy-start | bytes 388
  165.6 36.2 %copy-start.4 = (bf16[1,512,1,128]{1,3,2,0:T(8,128)(2,1)S(1)}, bf16[1,512,1,128]{1,3,2,0:T(8,128)(2,1)}, u32[]{:S(2)}) copy-start(bf16[1,512,1,128]{1,3,2,0:T(8,128)(2,1)} %fusion.23) | copy-start | bytes 393220
Sparse Core Ops, SparseCore 0:
  10.6 149.8 all-gather.1
  204.7 32.2 reduce-scatter.1
